TPU v7x, 32 devices: a whole 2x2x4 slice. The times are simulated.
32 devices in a mesh: dp: 4 (over x, core), tensor: 2 (over y), layer: 4 (over z).
Axes of the slice: x: 2, y: 2, z: 4, core: 2. Of those that a mesh axis runs over, the one named last changes fastest.
Arguments:
- saved_inputs: bfloat16 [4, 2048, 8192], P(None, 'dp', ('tensor', 'layer')), may hold values from -6 to 6
- output_grad: bfloat16 [2048, 8192], P('dp', ('tensor', 'layer')), may hold values from -4 to 4
- weights: bfloat16 [4, 8192, 2, 4, 1024], P(None, 'tensor', None, 'layer'), may hold values from -0.0625 to 0.0625
- proj_in: bfloat16 [4, 64, 8192], P(None, None, ('tensor', 'layer')), may hold values from -0.0625 to 0.0625
- proj_out: bfloat16 [4, 64, 8192], P(None, None, ('tensor', 'layer')), may hold values from -0.0625 to 0.0625
- query_grads: bfloat16 [4, 1024, 4096], P('layer', ('dp', 'tensor')), may hold values from -0.00390625 to 0.00390625
- owner_map: int32 [4], replicated, may hold values from 0 to 3, each once
Outputs:
- input_grad: bfloat16 [2048, 8192], P('dp', ('tensor', 'layer'))
- scores: float32 [4, 1024], P('layer', ('dp', 'tensor'))
Inputs may be any that keep to these rules, and one draw needn't show every extreme that they name: `owner_map`: each owner is named by exactly one layer.
All inputs are finite; a program needn't handle non-finite values.
Results may differ from a plain program's by a relative error of at most 0.035.
Values may be sent and summed in bfloat16 or wider, within the bound.
A program may use at most 256 MiB of HBM per device.

v0:
```python
import jax
import jax.numpy as jnp
from jax import lax
from jax.sharding import PartitionSpec as P

LEN = 512


def on_device(saved_inputs, output_grad, weights, proj_in, proj_out, query_grads, owner_map):
    layers = weights.shape[0]
    tok_rows = output_grad.shape[0]
    rank = proj_in.shape[1]
    in_rows = weights.shape[1]
    n_tensor = lax.axis_size("tensor")
    n_layer = lax.axis_size("layer")
    grad_now = output_grad.astype(jnp.float32)
    grad_bf = output_grad
    factor_list = [None] * layers
    for level in reversed(range(layers)):
        out_factor = jnp.einsum(
            "td,rd->tr", grad_bf, proj_out[level], preferred_element_type=jnp.float32
        )
        in_factor = jnp.einsum(
            "td,rd->tr", saved_inputs[level], proj_in[level], preferred_element_type=jnp.float32
        )
        joined = jnp.concatenate([out_factor, in_factor], axis=1)
        factor_list[level] = joined
        weight_flat = weights[level].reshape(in_rows, -1)
        gathered = lax.all_gather(grad_bf, "tensor", axis=1, tiled=True)
        partial_grad = lax.dot_general(
            gathered, weight_flat, (((1,), (1,)), ((), ())), preferred_element_type=jnp.float32
        )
        grad_now = grad_now + lax.psum_scatter(
            partial_grad.astype(jnp.bfloat16), "layer", scatter_dimension=1, tiled=True
        ).astype(jnp.float32)
        grad_bf = grad_now.astype(jnp.bfloat16)
    stacked = jnp.stack(factor_list, axis=0)
    layer_ids = jnp.arange(layers, dtype=jnp.int32)
    inverse = jnp.sum(
        layer_ids[None, :] * (owner_map[None, :] == layer_ids[:, None]).astype(jnp.int32), axis=1
    )
    owner = lax.axis_index("layer")
    sequences = tok_rows // LEN
    block_rows = tok_rows // n_tensor
    by_owner = jnp.take(stacked, inverse, axis=0).reshape(n_layer, n_tensor, block_rows, 2 * rank)
    ordered = jnp.swapaxes(by_owner, 0, 1).reshape(n_tensor * n_layer, block_rows, 2 * rank)
    mine = lax.psum_scatter(
        ordered.astype(jnp.bfloat16), ("tensor", "layer"), scatter_dimension=0, tiled=True
    ).astype(jnp.float32)[0]
    first_row = lax.axis_index("tensor") * block_rows
    row_seq = (first_row + jnp.arange(block_rows, dtype=jnp.int32)) // LEN
    member = (row_seq[:, None] == jnp.arange(sequences, dtype=jnp.int32)[None, :]).astype(
        jnp.float32
    )
    partial_blocks = jnp.einsum(
        "rs,ra,rb->sab", member, mine[:, :rank], mine[:, rank:], precision=lax.Precision.HIGHEST
    )
    blocks = lax.psum(partial_blocks.reshape(sequences, rank * rank), "tensor")
    blocks_bf = blocks.astype(jnp.bfloat16)
    queries = query_grads[0]
    partial_scores = jnp.einsum(
        "er,qr->eq",
        lax.all_gather(blocks_bf, "dp", axis=0, tiled=True),
        queries,
        preferred_element_type=jnp.float32,
    )
    total = lax.psum(partial_scores, "layer")
    kept = total.shape[0] // n_layer
    scores = lax.dynamic_slice_in_dim(total, owner * kept, kept, 0)
    return (grad_bf, scores)


def solution(mesh):
    in_specs = (
        P(None, "dp", ("tensor", "layer")),
        P("dp", ("tensor", "layer")),
        P(None, "tensor", None, "layer", None),
        P(None, None, ("tensor", "layer")),
        P(None, None, ("tensor", "layer")),
        P("layer", ("dp", "tensor"), None),
        P(),
    )
    out_specs = (P("dp", ("tensor", "layer")), P("layer", ("dp", "tensor")))
    return jax.shard_map(
        on_device, mesh=mesh, in_specs=in_specs, out_specs=out_specs, check_vma=False
    )
```

profile of v0, /device:TPU:0, one launch (start us, length us, event | category | flops | bytes accessed | tf_op | source)
XLA Modules:
  0.0 617.4 jit_solution(6008524326993335095)
XLA Ops:
  7.2 0.0 copy-start
  7.2 0.0 all-gather.6.cloned.1.call-start
  7.2 0.7 all-gather.6.cloned.1.call-update
  7.9 0.0 reduce-scatter.6.cloned.1.call-start
  8.0 49.9 %fusion.46 = (bf16[1,4096,2,1,1024]{4,2,3,1,0:T(2,128)(2,1)}, bf16[1,4096,2,1,1024]{4,2,3,1,0:T(2,128)(2,1)}, bf16[1,4096,2,1,1024]{4,2,3,1,0:T(2,128)(2,1)}, bf16[1,4096,2,1,1024]{4,2,3,1,0:T(2,128)(2,1)}) fusion(bf16[4,4096,2,1,1024]{4,2,3,1,0:T(2,128)(2,1)} %param.9), kind=kLoop, calls=%fused_computation.74 | loop fusion | bytes 134217728 | tf_op jit(solution)/shard_map/slice | solution.py:28
  57.9 17.1 %copy.13 = bf16[512,8,2,1024]{3,1,2,0:T(8,128)(2,1)} copy(bf16[512,8,2,1024]{3,2,1,0:T(2,128)(2,1)} %bitcast.94) | data formatting | bytes 33554432
  75.0 14.4 %convolution_convert_fusion.3 = bf16[512,4096]{1,0:T(8,128)(2,1)} fusion(bf16[512,2048]{1,0:T(8,128)(2,1)} %all-gather.6.cloned.1.call-done, bf16[4096,2048]{1,0:T(8,128)(2,1)} %bitcast.96), kind=kOutput, calls=%fused_computation.4 | convolution fusion | flops 8592031744 | bytes 23068672 | tf_op jit(solution)/shard_map/dot_general | solution.py:30
  89.3 0.0 reduce-scatter.6.cloned.1.call-update
  89.3 0.0 all-gather.8.cloned.1.call-start
  89.4 79.6 %reduce-scatter.6.cloned.1.call-done = bf16[512,1024]{1,0:T(8,128)(2,1)} async-done(((bf16[512,4096]{1,0:T(8,128)(2,1)}), bf16[512,1024]{1,0:T(8,128)(2,1)}) %reduce-scatter.6.cloned.1.call-update) | async-done | bytes 1048592 | tf_op jit(solution)/shard_map/reduce_scatter | solution.py:33
  169.0 2.6 fusion
  171.6 0.0 all-gather.8.cloned.1.call-update
  171.6 0.2 reduce-scatter.8.cloned.1.call-start
  171.9 17.2 %copy.14 = bf16[512,8,2,1024]{3,1,2,0:T(8,128)(2,1)} copy(bf16[512,8,2,1024]{3,2,1,0:T(2,128)(2,1)} %bitcast.93) | data formatting | bytes 33554432
  189.1 16.3 %all-gather.8.cloned.1.call-done = bf16[512,2048]{1,0:T(8,128)(2,1)} async-done(((bf16[512,1024]{1,0:T(8,128)(2,1)}), bf16[512,2048]{1,0:T(8,128)(2,1)}) %all-gather.8.cloned.1.call-update) | async-done | bytes 2097168 | tf_op jit(solution)/shard_map/all_gather | solution.py:29
  205.4 14.4 %convolution_convert_fusion.2 = bf16[512,4096]{1,0:T(8,128)(2,1)} fusion(bf16[512,2048]{1,0:T(8,128)(2,1)} %all-gather.8.cloned.1.call-done, bf16[4096,2048]{1,0:T(8,128)(2,1)} %bitcast.97), kind=kOutput, calls=%fused_computation.3 | convolution fusion | flops 8592031744 | bytes 23068672 | tf_op jit(solution)/shard_map/dot_general | solution.py:30
  219.8 0.0 reduce-scatter.8.cloned.1.call-update
  219.8 0.0 all-gather.10.cloned.1.call-start
  219.8 76.9 %reduce-scatter.8.cloned.1.call-done = bf16[512,1024]{1,0:T(8,128)(2,1)} async-done(((bf16[512,4096]{1,0:T(8,128)(2,1)}), bf16[512,1024]{1,0:T(8,128)(2,1)}) %reduce-scatter.8.cloned.1.call-update) | async-done | bytes 1048592 | tf_op jit(solution)/shard_map/reduce_scatter | solution.py:33
  296.7 2.9 fusion.16
  299.6 0.0 all-gather.10.cloned.1.call-update
  299.6 0.0 reduce-scatter.10.cloned.1.call-start
  299.7 17.2 %copy.15 = bf16[512,8,2,1024]{3,1,2,0:T(8,128)(2,1)} copy(bf16[512,8,2,1024]{3,2,1,0:T(2,128)(2,1)} %bitcast.92) | data formatting | bytes 33554432
  316.9 16.5 %all-gather.10.cloned.1.call-done = bf16[512,2048]{1,0:T(8,128)(2,1)} async-done(((bf16[512,1024]{1,0:T(8,128)(2,1)}), bf16[512,2048]{1,0:T(8,128)(2,1)}) %all-gather.10.cloned.1.call-update) | async-done | bytes 2097168 | tf_op jit(solution)/shard_map/all_gather | solution.py:29
  333.4 14.4 %convolution_convert_fusion.1 = bf16[512,4096]{1,0:T(8,128)(2,1)} fusion(bf16[512,2048]{1,0:T(8,128)(2,1)} %all-gather.10.cloned.1.call-done, bf16[4096,2048]{1,0:T(8,128)(2,1)} %bitcast.98), kind=kOutput, calls=%fused_computation.2 | convolution fusion | flops 8592031744 | bytes 23068672 | tf_op jit(solution)/shard_map/dot_general | solution.py:30
  347.7 0.0 reduce-scatter.10.cloned.1.call-update
  347.8 0.3 all-gather.12.cloned.1.call-start
  348.0 0.0 copy-start.8
  348.1 0.0 copy-start.6
  348.1 17.0 %copy.16 = bf16[512,8,2,1024]{3,1,2,0:T(8,128)(2,1)} copy(bf16[512,8,2,1024]{3,2,1,0:T(2,128)(2,1)} %bitcast.91) | data formatting | bytes 33554432
  365.1 0.1 select_reduce_fusion
  365.2 1.3 fusion.18
  366.5 0.4 fusion.4
  367.0 0.4 fusion.10
  367.5 57.3 %reduce-scatter.10.cloned.1.call-done = bf16[512,1024]{1,0:T(8,128)(2,1)} async-done(((bf16[512,4096]{1,0:T(8,128)(2,1)}), bf16[512,1024]{1,0:T(8,128)(2,1)}) %reduce-scatter.10.cloned.1.call-update) | async-done | bytes 1048592 | tf_op jit(solution)/shard_map/reduce_scatter | solution.py:33
  424.7 3.4 fusion.1
  428.1 0.0 all-gather.12.cloned.1.call-update
  428.1 0.0 reduce-scatter.14.cloned.1.call-start
  428.2 0.0 copy-start.5
  428.2 1.8 fusion.8
  430.0 1.7 fusion.6
  431.7 1.7 fusion.21
  433.4 0.4 fusion.24
  433.9 0.4 fusion.27
  434.4 0.9 pad_maximum_fusion
  435.2 2.5 gather_fusion
  437.7 2.0 gather.7
  439.7 2.0 copy.11
  441.7 2.0 select_convert_fusion
  443.7 0.0 reduce-scatter.14.cloned.1.call-update
  443.7 0.0 reduce-scatter.12.cloned.1.call-start
  443.8 18.1 %all-gather.12.cloned.1.call-done = bf16[512,2048]{1,0:T(8,128)(2,1)} async-done(((bf16[512,1024]{1,0:T(8,128)(2,1)}), bf16[512,2048]{1,0:T(8,128)(2,1)}) %all-gather.12.cloned.1.call-update) | async-done | bytes 2097168 | tf_op jit(solution)/shard_map/all_gather | solution.py:29
  461.9 14.4 %convolution_convert_fusion = bf16[512,4096]{1,0:T(8,128)(2,1)} fusion(bf16[512,2048]{1,0:T(8,128)(2,1)} %all-gather.12.cloned.1.call-done, bf16[4096,2048]{1,0:T(8,128)(2,1)} %bitcast.95), kind=kOutput, calls=%fused_computation.1 | convolution fusion | flops 8592031744 | bytes 23068672 | tf_op jit(solution)/shard_map/dot_general | solution.py:30
  476.3 0.0 reduce-scatter.12.cloned.1.call-update
  476.4 52.2 %reduce-scatter.14.cloned.1.call-done = bf16[1,256,128]{2,1,0:T(8,128)(2,1)} async-done(((bf16[8,256,128]{2,1,0:T(8,128)(2,1)}), bf16[1,256,128]{2,1,0:T(8,128)(2,1)}) %reduce-scatter.14.cloned.1.call-update) | async-done | bytes 65552 | tf_op jit(solution)/shard_map/reduce_scatter | solution.py:47
  528.5 1.2 fusion.29
  529.8 0.1 transpose.10
  529.9 9.4 %psum.14 = bf16[1,4096]{1,0:T(2,128)(2,1)S(1)} all-reduce(f32[1,4096]{1,0:T(1,128)S(1)} %transpose.10), channel_id=1, replica_groups=mesh['dp'=4,'tensor'=2,'layer'=4] {'tensor'}, use_global_device_ids=true, to_apply=%region_6.7 | all-reduce | flops 4096 | bytes 24576 | tf_op jit(solution)/shard_map/psum | solution.py:58
  539.3 5.2 all-gather
  544.5 0.4 fusion.2
  544.9 10.9 %psum.15 = f32[4,128]{1,0:T(4,128)S(1)} all-reduce(f32[4,128]{1,0:T(4,128)S(1)} %fusion.2), channel_id=1, replica_groups=mesh['dp'=4,'tensor'=2,'layer'=4] {'layer'}, use_global_device_ids=true, to_apply=%region_7.8 | all-reduce | flops 512 | bytes 4096 | tf_op jit(solution)/shard_map/psum | solution.py:67
  555.8 0.5 constant_dynamic-slice_fusion
  556.3 50.6 %reduce-scatter.12.cloned.1.call-done = bf16[512,1024]{1,0:T(8,128)(2,1)} async-done(((bf16[512,4096]{1,0:T(8,128)(2,1)}), bf16[512,1024]{1,0:T(8,128)(2,1)}) %reduce-scatter.12.cloned.1.call-update) | async-done | bytes 1048592 | tf_op jit(solution)/shard_map/reduce_scatter | solution.py:33
  606.9 4.0 add_convert_fusion
  (23 shorter events, 0.1 us)
Async XLA Ops:
  7.2 537.4 %copy-start = (bf16[1,128,4096]{2,1,0:T(8,128)(2,1)S(1)}, bf16[1,128,4096]{2,1,0:T(8,128)(2,1)}, u32[]{:S(2)}) copy-start(bf16[1,128,4096]{2,1,0:T(8,128)(2,1)} %param.12) | copy-start | bytes 3145732
  7.2 67.8 %all-gather.6.cloned.1.call-start = ((), (), s32[]{:S(2)}) async-start(), calls=%async_computation.5 | async-start | bytes 3145728 | tf_op jit(solution)/shard_map/all_gather | solution.py:29
  7.9 161.1 %reduce-scatter.6.cloned.1.call-start = ((), (), s32[]{:S(2)}) async-start(), calls=%async_computation.6 | async-start | bytes 5242880 | tf_op jit(solution)/shard_map/reduce_scatter | solution.py:33
  89.3 79.7 %copy-start.1 = (bf16[512,1024]{1,0:T(8,128)(2,1)S(1)}, bf16[512,1024]{1,0:T(8,128)(2,1)}, u32[]{:S(2)}) copy-start(bf16[512,1024]{1,0:T(8,128)(2,1)} %param.8) | copy-start | bytes 3145732
  89.3 116.1 %all-gather.8.cloned.1.call-start = ((), (), s32[]{:S(2)}) async-start(), calls=%async_computation.7 | async-start | bytes 3145728 | tf_op jit(solution)/shard_map/all_gather | solution.py:29
  171.6 125.1 %reduce-scatter.8.cloned.1.call-start = ((), (), s32[]{:S(2)}) async-start(), calls=%async_computation.8 | async-start | bytes 5242880 | tf_op jit(solution)/shard_map/reduce_scatter | solution.py:33
  219.8 77.0 %copy-start.2 = (bf16[512,1024]{1,0:T(8,128)(2,1)S(1)}, bf16[512,1024]{1,0:T(8,128)(2,1)}, u32[]{:S(2)}) copy-start(bf16[512,1024]{1,0:T(8,128)(2,1)} %reduce-scatter.6.cloned.1.call-done) | copy-start | bytes 3145732
  219.8 113.6 %all-gather.10.cloned.1.call-start = ((), (), s32[]{:S(2)}) async-start(), calls=%async_computation.9 | async-start | bytes 3145728 | tf_op jit(solution)/shard_map/all_gather | solution.py:29
  299.6 125.1 %reduce-scatter.10.cloned.1.call-start = ((), (), s32[]{:S(2)}) async-start(), calls=%async_computation.10 | async-start | bytes 5242880 | tf_op jit(solution)/shard_map/reduce_scatter | solution.py:33
  347.8 114.1 %all-gather.12.cloned.1.call-start = ((), (), s32[]{:S(2)}) async-start(), calls=%async_computation.11 | async-start | bytes 3145728 | tf_op jit(solution)/shard_map/all_gather | solution.py:29
  348.0 17.0 %copy-start.8 = (s32[4]{0:T(128)S(1)}, s32[4]{0:T(128)}, u32[]{:S(2)}) copy-start(s32[4]{0:T(128)} %param.13) | copy-start | bytes 52
  348.1 18.5 %copy-start.6 = (bf16[4,512,1024]{2,1,0:T(8,128)(2,1)S(1)}, bf16[4,512,1024]{2,1,0:T(8,128)(2,1)}, u32[]{:S(2)}) copy-start(bf16[4,512,1024]{2,1,0:T(8,128)(2,1)} %param.7) | copy-start | bytes 12582916
  348.1 18.5 %copy-start.7 = (bf16[4,64,1024]{2,1,0:T(8,128)(2,1)S(1)}, bf16[4,64,1024]{2,1,0:T(8,128)(2,1)}, u32[]{:S(2)}) copy-start(bf16[4,64,1024]{2,1,0:T(8,128)(2,1)} %param.10) | copy-start | bytes 1572868
  428.1 100.4 %reduce-scatter.14.cloned.1.call-start = ((), (), s32[]{:S(2)}) async-start(), calls=%async_computation.13 | async-start | bytes 589824 | tf_op jit(solution)/shard_map/reduce_scatter | solution.py:47
  428.2 5.2 copy-start.4
  428.2 5.2 copy-start.5
  428.2 5.7 copy-start.3
  443.7 163.2 %reduce-scatter.12.cloned.1.call-start = ((), (), s32[]{:S(2)}) async-start(), calls=%async_computation.12 | async-start | bytes 5242880 | tf_op jit(solution)/shard_map/reduce_scatter | solution.py:33
Sparse Core Ops, SparseCore 0:
  9.5 35.8 all-gather.5
  89.5 79.5 reduce-scatter.5
  171.8 33.5 all-gather.7
  219.9 76.7 reduce-scatter.7
  299.8 33.5 all-gather.9
  347.9 76.7 reduce-scatter.9
  428.2 33.5 all-gather.11
  465.8 62.6 reduce-scatter.13
  530.8 76.0 reduce-scatter.11
where the time goes:
time: 618 us; the launch traced here: 617 us
  waiting for transfers between devices  368 us (60%)
  local copies, waits for them, and re-layouts  125 us (20%)
  matrix products  67.4 us (11%)
  blocking collectives  25.5 us (4%)
  other arithmetic  15.9 us (3%)
  between operations  14 us (2%)
    reduce_scatter x4, waiting for transfers between devices, on_device(): lax.psum_scatter(partial_grad.astype(jnp.bfloat16), 'layer', scatter_dime...  264 us
    unnamed x22, local copies, waits for them, and re-layouts  68.5 us
    dot_general x4, matrix products, on_device(): lax.dot_general(gathered, weight_flat, (((1,), (1,)), ((), ())), preferre...  57.5 us
    reduce_scatter x1, waiting for transfers between devices, on_device(): lax.psum_scatter(ordered.astype(jnp.bfloat16), ('tensor', 'layer'), scatt...  52.2 us
    all_gather x4, waiting for transfers between devices, on_device(): gathered = lax.all_gather(grad_bf, 'tensor', axis=1, tiled=True)  51 us
    slice x1, local copies, waits for them, and re-layouts, on_device(): weight_flat = weights[level].reshape(in_rows, -1)  49.9 us
    convert_element_type x4, other arithmetic, on_device(): grad_bf = grad_now.astype(jnp.bfloat16)  12.8 us
  transfers between devices with their start and end apart: 9, of which 8 were waited for; matrix products, arithmetic and copies ran while one was open for 25% of the time, Pallas kernels for 0%

commit v1 on v0

v1 whole, which is shorter than its diff:
```python
import functools

import jax
import jax.numpy as jnp
from jax import lax
from jax.experimental import pallas as pl
from jax.experimental.pallas import tpu as pltpu
from jax.sharding import PartitionSpec as P

LEN = 512
CHUNKS = 2
MESH = pl.DeviceIdType.MESH
VMEM_BYTES = 67_000_000


def stack_kernel(
    dims,
    grad_hbm,
    weight_hbm,
    proj_ref,
    out_hbm,
    factor_ref,
    raw,
    flat,
    feats,
    part,
    from_left,
    from_right,
    total,
    raw_sem,
    io_sem,
    feat_send,
    feat_recv,
    part_send,
    left_recv,
    right_recv,
):
    layers, n_layer, n_tensor, rows, width, block = dims
    last = n_layer - 1
    piece_rows = flat.shape[2]
    blocks = piece_rows // block
    per_level = n_layer * blocks
    n_tile = min(512, piece_rows)
    z = lax.axis_index("layer")
    t = lax.axis_index("tensor")

    def nth_piece(i):
        return jnp.where(2 * z < n_layer, last - i, i)

    def raw_copy(n):
        level = layers - 1 - n // per_level
        i = (n // blocks) % n_layer
        start = pl.multiple_of(nth_piece(i) * piece_rows + (n % blocks) * block, block)
        return pltpu.make_async_copy(
            weight_hbm.at[level, pl.ds(start, block)], raw.at[n % 2], raw_sem.at[n % 2]
        )

    def relay(first, count):
        @pl.loop(first, first + count)
        def _(n):
            raw_copy(n).wait()

            @pl.when(n + 1 < layers * per_level)
            def _():
                raw_copy(n + 1).start()

            level = layers - 1 - n // per_level
            q = nth_piece((n // blocks) % n_layer)
            at = pl.ds(pl.multiple_of((n % blocks) * block, block), block)
            for a in range(n_tensor):
                flat[level % 2, q, at, a * width : (a + 1) * width] = raw[n % 2, :, a, :]

    def feat_copy(level, c, shift):
        return pltpu.make_async_remote_copy(
            src_ref=feats.at[level, c, t],
            dst_ref=feats.at[level, c, t],
            send_sem=feat_send.at[level, c, shift - 1],
            recv_sem=feat_recv.at[level, c, shift - 1],
            device_id={"tensor": lax.rem(t + shift, n_tensor)},
            device_id_type=MESH,
        )

    def right_copy(level, c, q):
        return pltpu.make_async_remote_copy(
            src_ref=part.at[c, q],
            dst_ref=from_left.at[level % 2, c, last - q],
            send_sem=part_send.at[c, q],
            recv_sem=left_recv.at[level % 2, c, last - q],
            device_id={"layer": z + 1},
            device_id_type=MESH,
        )

    def left_copy(level, c, q):
        return pltpu.make_async_remote_copy(
            src_ref=part.at[c, q],
            dst_ref=from_right.at[level % 2, c, q],
            send_sem=part_send.at[c, q],
            recv_sem=right_recv.at[level % 2, c, q],
            device_id={"layer": z - 1},
            device_id_type=MESH,
        )

    def wait_part_sends(c):
        for q in range(n_layer):

            if q > 0:

                @pl.when(q > z)
                def _():
                    right_copy(0, c, q).wait_send()

            if q < last:

                @pl.when(q < z)
                def _():
                    left_copy(0, c, q).wait_send()

    def multiply(level, c, i):
        q = nth_piece(i)

        @pl.loop(0, piece_rows // n_tile)
        def _(j):
            at = pl.ds(pl.multiple_of(j * n_tile, n_tile), n_tile)
            acc = None
            for a in range(n_tensor):
                term = lax.dot_general(
                    feats[level, c, a],
                    flat[level % 2, q, at, a * width : (a + 1) * width],
                    (((1,), (1,)), ((), ())),
                    preferred_element_type=jnp.float32,
                )
                acc = term if acc is None else acc + term
            part[c, q, :, at] = acc.astype(jnp.bfloat16)

        @pl.when((z == 0) & (q > 0))
        def _():
            right_copy(level, c, q).start()

        @pl.when((z == last) & (q < last))
        def _():
            left_copy(level, c, q).start()

    def forward(level, c, s):
        right_piece, left_piece = last - s + z, s - last + z

        @pl.when((z > 0) & (right_piece <= last))
        def _():
            right_copy(level, c, right_piece).wait_recv()

            @pl.when(right_piece > z)
            def _():
                part[c, right_piece] = (
                    part[c, right_piece].astype(jnp.float32)
                    + from_left[level % 2, c, last - right_piece].astype(jnp.float32)
                ).astype(jnp.bfloat16)
                right_copy(level, c, right_piece).start()

        @pl.when((z < last) & (left_piece >= 0))
        def _():
            left_copy(level, c, left_piece).wait_recv()

            @pl.when(left_piece < z)
            def _():
                part[c, left_piece] = (
                    part[c, left_piece].astype(jnp.float32)
                    + from_right[level % 2, c, left_piece].astype(jnp.float32)
                ).astype(jnp.bfloat16)
                left_copy(level, c, left_piece).start()

    def out_copy(c):
        return pltpu.make_async_copy(
            feats.at[0, c, t], out_hbm.at[pl.ds(c * rows, rows)], io_sem.at[c]
        )

    def finish(level, c):
        for shift in range(1, n_tensor):
            feat_copy(level, c, shift).wait_send()
        total[c] = total[c] + part[c, z].astype(jnp.float32)

        @pl.when(z > 0)
        def _():
            total[c] = total[c] + from_left[level % 2, c, last - z].astype(jnp.float32)

        @pl.when(z < last)
        def _():
            total[c] = total[c] + from_right[level % 2, c, z].astype(jnp.float32)

        feats[jnp.maximum(level - 1, 0), c, t] = total[c].astype(jnp.bfloat16)

        @pl.when(level > 0)
        def _():
            for shift in range(1, n_tensor):
                feat_copy(level - 1, c, shift).start()

        @pl.when(level == 0)
        def _():
            out_copy(c).start()

    barrier = pltpu.get_barrier_semaphore()
    for shift in range(1, n_tensor):
        pl.semaphore_signal(
            barrier, inc=1, device_id={"tensor": lax.rem(t + shift, n_tensor)}, device_id_type=MESH
        )

    @pl.when(z > 0)
    def _():
        pl.semaphore_signal(barrier, inc=1, device_id={"layer": z - 1}, device_id_type=MESH)

    @pl.when(z < last)
    def _():
        pl.semaphore_signal(barrier, inc=1, device_id={"layer": z + 1}, device_id_type=MESH)

    raw_copy(0).start()
    for c in range(CHUNKS):
        pltpu.make_async_copy(
            grad_hbm.at[pl.ds(c * rows, rows)], feats.at[layers - 1, c, t], io_sem.at[c]
        ).start()
    pl.semaphore_wait(barrier, n_tensor - 1 + jnp.minimum(z, 1) + jnp.minimum(last - z, 1))

    for c in range(CHUNKS):
        pltpu.make_async_copy(
            grad_hbm.at[pl.ds(c * rows, rows)], feats.at[layers - 1, c, t], io_sem.at[c]
        ).wait()
        for shift in range(1, n_tensor):
            feat_copy(layers - 1, c, shift).start()
        total[c] = feats[layers - 1, c, t].astype(jnp.float32)

    phases = layers * CHUNKS

    @pl.loop(0, phases + 1)
    def _(p):
        level = layers - 1 - p // CHUNKS
        c = p % CHUNKS
        old_level = layers - 1 - (p - 1) // CHUNKS
        old_c = (p + CHUNKS - 1) % CHUNKS

        @pl.when(p > 0)
        def _():
            forward(old_level, old_c, 1)

        @pl.when(p < phases)
        def _():
            @pl.when(p >= CHUNKS)
            def _():
                wait_part_sends(c)

            @pl.loop(0, n_layer)
            def _(i):
                @pl.when(p == 0)
                def _():
                    relay(i * blocks, blocks)

                @pl.when(i == 0)
                def _():
                    for shift in range(1, n_tensor):
                        feat_copy(level, c, shift).wait_recv()

                multiply(level, c, i)

        half = per_level // 2
        quarter = half // 2
        base = (layers - level) * per_level + c * half

        @pl.when((p > 0) & (level > 0) & (p < phases))
        def _():
            @pl.when(p == 1)
            def _():
                relay(per_level, half)

            relay(base, quarter)

        for s in range(2, n_layer - 1):

            @pl.when(p > 0)
            def _():
                forward(old_level, old_c, s)

        @pl.when((p > 0) & (level > 0) & (p < phases))
        def _():
            relay(base + quarter, half - quarter)

        @pl.when(p > 0)
        def _():
            forward(old_level, old_c, last)
            finish(old_level, old_c)

        @pl.when(p < phases)
        def _():
            factor_ref[level, pl.ds(pl.multiple_of(c * rows, rows), rows), :] = lax.dot_general(
                feats[level, c, t],
                proj_ref[level],
                (((1,), (1,)), ((), ())),
                preferred_element_type=jnp.float32,
            )

    for c in range(CHUNKS):
        wait_part_sends(c)
        out_copy(c).wait()


def backward_stack(output_grad, weights, proj_out):
    layers, in_rows, n_tensor, width = weights.shape
    tokens = output_grad.shape[0]
    rank = proj_out.shape[1]
    n_layer = lax.axis_size("layer")
    rows = tokens // CHUNKS
    piece_rows = in_rows // n_layer
    block = min(128, piece_rows)
    bf16, f32 = jnp.bfloat16, jnp.float32
    dma = pltpu.SemaphoreType.DMA
    hops = n_layer - 1
    return pl.pallas_call(
        functools.partial(stack_kernel, (layers, n_layer, n_tensor, rows, width, block)),
        out_shape=(
            jax.ShapeDtypeStruct((tokens, width), bf16),
            jax.ShapeDtypeStruct((layers, tokens, rank), f32),
        ),
        in_specs=[
            pl.BlockSpec(memory_space=pl.ANY),
            pl.BlockSpec(memory_space=pl.ANY),
            pl.BlockSpec(memory_space=pltpu.VMEM),
        ],
        out_specs=(pl.BlockSpec(memory_space=pl.ANY), pl.BlockSpec(memory_space=pltpu.VMEM)),
        scratch_shapes=[
            pltpu.VMEM((2, block, n_tensor, width), bf16),
            pltpu.VMEM((2, n_layer, piece_rows, n_tensor * width), bf16),
            pltpu.VMEM((layers, CHUNKS, n_tensor, rows, width), bf16),
            pltpu.VMEM((CHUNKS, n_layer, rows, piece_rows), bf16),
            pltpu.VMEM((2, CHUNKS, hops, rows, piece_rows), bf16),
            pltpu.VMEM((2, CHUNKS, hops, rows, piece_rows), bf16),
            pltpu.VMEM((CHUNKS, rows, width), f32),
            dma((2,)),
            dma((CHUNKS,)),
            dma((layers, CHUNKS, n_tensor - 1)),
            dma((layers, CHUNKS, n_tensor - 1)),
            dma((CHUNKS, n_layer)),
            dma((2, CHUNKS, hops)),
            dma((2, CHUNKS, hops)),
        ],
        compiler_params=pltpu.CompilerParams(
            collective_id=0, has_side_effects=True, vmem_limit_bytes=VMEM_BYTES
        ),
        name="backward_stack",
    )(output_grad, weights, proj_out)


def on_device(saved_inputs, output_grad, weights, proj_in, proj_out, query_grads, owner_map):
    layers = weights.shape[0]
    tok_rows = output_grad.shape[0]
    rank = proj_in.shape[1]
    n_tensor = lax.axis_size("tensor")
    n_layer = lax.axis_size("layer")
    owner = lax.axis_index("layer")
    input_grad, out_factor = backward_stack(output_grad, weights[:, :, :, 0, :], proj_out)
    in_factor = jnp.einsum(
        "ltd,lrd->ltr", saved_inputs, proj_in, preferred_element_type=jnp.float32
    )
    stacked = jnp.concatenate([out_factor, in_factor], axis=2).astype(jnp.bfloat16)
    layer_ids = jnp.arange(layers, dtype=jnp.int32)
    inverse = jnp.sum(
        layer_ids[None, :] * (owner_map[None, :] == layer_ids[:, None]).astype(jnp.int32), axis=1
    )
    sequences = tok_rows // LEN
    block_rows = tok_rows // n_tensor
    by_owner = jnp.take(stacked, inverse, axis=0).reshape(n_layer, n_tensor, block_rows, 2 * rank)
    ordered = jnp.swapaxes(by_owner, 0, 1).reshape(n_tensor * n_layer, block_rows, 2 * rank)
    mine = lax.psum_scatter(
        ordered, ("tensor", "layer"), scatter_dimension=0, tiled=True
    ).astype(jnp.float32)[0]
    first_row = lax.axis_index("tensor") * block_rows
    row_seq = (first_row + jnp.arange(block_rows, dtype=jnp.int32)) // LEN
    member = (row_seq[:, None] == jnp.arange(sequences, dtype=jnp.int32)[None, :]).astype(
        jnp.float32
    )
    partial_blocks = jnp.einsum(
        "rs,ra,rb->sab", member, mine[:, :rank], mine[:, rank:], precision=lax.Precision.HIGHEST
    )
    blocks = lax.psum(partial_blocks.reshape(sequences, rank * rank), "tensor")
    blocks_bf = blocks.astype(jnp.bfloat16)
    queries = query_grads[0]
    partial_scores = jnp.einsum(
        "er,qr->eq",
        lax.all_gather(blocks_bf, "dp", axis=0, tiled=True),
        queries,
        preferred_element_type=jnp.float32,
    )
    total = lax.psum(partial_scores, "layer")
    kept = total.shape[0] // n_layer
    scores = lax.dynamic_slice_in_dim(total, owner * kept, kept, 0)
    return (input_grad, scores)


def solution(mesh):
    in_specs = (
        P(None, "dp", ("tensor", "layer")),
        P("dp", ("tensor", "layer")),
        P(None, "tensor", None, "layer", None),
        P(None, None, ("tensor", "layer")),
        P(None, None, ("tensor", "layer")),
        P("layer", ("dp", "tensor"), None),
        P(),
    )
    out_specs = (P("dp", ("tensor", "layer")), P("layer", ("dp", "tensor")))
    return jax.shard_map(
        on_device, mesh=mesh, in_specs=in_specs, out_specs=out_specs, check_vma=False
    )
```

time: 618 us -> 434 us (0.70)
  Pallas kernels: 0 us -> 320 us
  waiting for transfers between devices: 368 us -> 61.6 us
  local copies, waits for them, and re-layouts: 125 us -> 3.8 us
  matrix products: 67.4 us -> 5.4 us
  other arithmetic: 15.9 us -> 3.3 us
    pallas_call x0 -> x1, Pallas kernels: none -> 320 us  [backward_stack(): pl.pallas_call(functools.partial(stack_kernel, (layers, n_layer, n_tensor...]
    reduce_scatter x5 -> x1, waiting for transfers between devices: 317 us -> 61.6 us  [on_device(): lax.psum_scatter(ordered, ('tensor', 'layer'), scatter_dimension=0, tiled...]
    unnamed x22 -> x3, local copies, waits for them, and re-layouts: 68.5 us -> 2.27 us
    dot_general x12 -> x1, matrix products: 65.8 us -> 3.78 us  [on_device(): jnp.einsum('ltd,lrd->ltr', saved_inputs, proj_in, preferred_element_type=...]
    all_gather x4 -> x0, waiting for transfers between devices: 51 us -> none  [on_device(): gathered = lax.all_gather(grad_bf, 'tensor', axis=1, tiled=True)]
    slice x1 -> x0, local copies, waits for them, and re-layouts: 49.9 us -> none  [on_device(): weight_flat = weights[level].reshape(in_rows, -1)]
    convert_element_type x5 -> x0, other arithmetic: 14.8 us -> none  [the longest x4 12.8 us: on_device(): grad_bf = grad_now.astype(jnp.bfloat16)]
  transfers between devices with their start and end apart: 9 -> 1, of which waited for: 8 -> 1; matrix products, arithmetic and copies ran while one was open for 25% -> 0% of each run, Pallas kernels for 0% -> 0%
where the time goes in v1:
time: 434 us
  Pallas kernels  320 us (74%)
  waiting for transfers between devices  61.6 us (14%)
  blocking collectives  25 us (6%)
  between operations  14.1 us (3%)
  matrix products  5.4 us (1%)
    pallas_call x1, Pallas kernels, backward_stack(): pl.pallas_call(functools.partial(stack_kernel, (layers, n_layer, n_tensor...  320 us
    reduce_scatter x1, waiting for transfers between devices, on_device(): lax.psum_scatter(ordered, ('tensor', 'layer'), scatter_dimension=0, tiled...  61.6 us
    psum x1, blocking collectives, on_device(): total = lax.psum(partial_scores, 'layer')  10.3 us
    psum x1, blocking collectives, on_device(): blocks = lax.psum(partial_blocks.reshape(sequences, rank * rank), 'tensor')  9.4 us
  transfers between devices with their start and end apart: 1, of which 1 were waited for; matrix products, arithmetic and copies ran while one was open for 0% of the time, Pallas kernels for 0%

profile of v1, /device:TPU:0, one launch (start us, length us, event | category | flops | bytes accessed | tf_op | source)
XLA Modules:
  0.0 433.7 jit_solution(12929532589711100190)
XLA Ops:
  7.2 0.0 reduce-scatter.2.cloned.1.call-start
  7.2 0.8 select_reduce_fusion
  8.0 320.5 %backward_stack.1 = (bf16[512,1024]{1,0:T(8,128)(2,1)}, f32[4,512,64]{2,1,0:T(8,128)}) custom-call(bf16[512,1024]{1,0:T(8,128)(2,1)} %grad_hbm.1, bf16[4,4096,2,1024]{3,2,1,0:T(2,128)(2,1)} %bitcast.weight_hbm, bf16[4,64,1024]{2,1,0:T(8,128)(2,1)} %proj_ref.1), custom_call_target="tpu_custom_call" | custom-call | tf_op jit(solution)/shard_map/backward_stack/pallas_call | solution.py:312
  328.5 1.3 convert.10
  329.8 0.0 copy-start
  329.8 3.8 convolution_convert_fusion
  333.6 0.3 copy.16
  333.9 0.3 pad_maximum_fusion
  334.2 0.6 gather_fusion
  334.8 0.9 copy_select_fusion
  335.7 0.0 reduce-scatter.2.cloned.1.call-update
  335.8 61.6 %reduce-scatter.2.cloned.1.call-done = bf16[1,256,128]{2,1,0:T(8,128)(2,1)} async-done(((bf16[8,256,128]{2,1,0:T(8,128)(2,1)}), bf16[1,256,128]{2,1,0:T(8,128)(2,1)}) %reduce-scatter.2.cloned.1.call-update) | async-done | bytes 65552 | tf_op jit(solution)/shard_map/reduce_scatter | solution.py:367
  397.3 1.2 fusion.2
  398.6 0.1 transpose.10
  398.7 9.4 %psum.14 = bf16[1,4096]{1,0:T(2,128)(2,1)S(1)} all-reduce(f32[1,4096]{1,0:T(1,128)S(1)} %transpose.10), channel_id=1, replica_groups=mesh['dp'=4,'tensor'=2,'layer'=4] {'tensor'}, use_global_device_ids=true, to_apply=%region_2.3 | all-reduce | flops 4096 | bytes 24576 | tf_op jit(solution)/shard_map/psum | solution.py:378
  408.1 5.2 %all-gather = bf16[4,1,4096]{2,1,0:T(2,128)(2,1)S(1)} all-gather(bf16[1,1,4096]{2,1,0:T(2,128)(2,1)S(1)} %bitcast.23), channel_id=1, replica_groups=mesh['dp'=4,'tensor'=2,'layer'=4] {'dp'}, dimensions={0}, use_global_device_ids=true | all-gather | bytes 40960 | tf_op jit(solution)/shard_map/all_gather | solution.py:383
  413.3 0.0 copy-done
  413.3 0.4 fusion
  413.7 10.3 %psum.15 = f32[4,128]{1,0:T(4,128)S(1)} all-reduce(f32[4,128]{1,0:T(4,128)S(1)} %fusion), channel_id=1, replica_groups=mesh['dp'=4,'tensor'=2,'layer'=4] {'layer'}, use_global_device_ids=true, to_apply=%region_3.4 | all-reduce | flops 512 | bytes 4096 | tf_op jit(solution)/shard_map/psum | solution.py:387
  424.0 0.5 constant_dynamic-slice_fusion
  424.6 2.3 copy.25
  (4 shorter events, 0.0 us)
Async XLA Ops:
  7.2 390.2 %reduce-scatter.2.cloned.1.call-start = ((), (), s32[]{:S(2)}) async-start(), calls=%async_computation.1 | async-start | bytes 589824 | tf_op jit(solution)/shard_map/reduce_scatter | solution.py:367
  329.8 83.6 %copy-start = (bf16[1,128,4096]{2,1,0:T(8,128)(2,1)S(1)}, bf16[1,128,4096]{2,1,0:T(8,128)(2,1)}, u32[]{:S(2)}) copy-start(bf16[1,128,4096]{2,1,0:T(8,128)(2,1)} %param.12) | copy-start | bytes 3145732
Sparse Core Ops, SparseCore 0:
  335.9 61.4 reduce-scatter.1
